TPU v7x, 128 devices: a whole 4x4x4 slice. The times are simulated.
128 devices in a mesh: lon: 32 (over y, z, x_lo), chan: 4 (over x_hi, core).
Axes of the slice: x: 4 (x_hi: 2, x_lo: 2; x = x_hi * 2 + x_lo), y: 4, z: 4, core: 2. Of those that a mesh axis runs over, the one named last changes fastest.
Arguments:
- fields: bfloat16 [1440, 49152], P('lon', 'chan'), may hold values from -6 to 6
- mix_weight: bfloat16 [384, 3456], P('chan'), may hold values from -0.109375 to 0.109375
- basis_values: float32 [5, 9, 65, 128], replicated, may hold values from -0.4 to 0.4
- source_rows: int32 [128, 5], replicated, may hold values from 0 to 131, as said below
- lon_reach: int32 [128, 5], replicated, may hold values from 1 to 32, as said below
- quad_weights: float32 [128], replicated, may hold values from 0.2 to 2
Outputs:
- spectrum: float32 [128, 552960], P('lon', 'chan')
Inputs may be any that keep to these rules, and one draw needn't show every extreme that they name: source_rows[i, e] lies between i + 4 - 4 and i + 8; entry 0 of row i is i + 4 and entry 1 is i + 4 - 4. `lon_reach`: every entry of the rows under 4 has reach 32.
All inputs are finite; a program needn't handle non-finite values.
Results may differ from a plain program's by a relative error of at most 0.005.
Values may be sent and summed in bfloat16 or wider, within the bound.
A program may use at most 128 MiB of HBM per device.

v0:
```python
import math

import jax
import jax.numpy as jnp
from jax import lax
from jax.sharding import PartitionSpec as P

C = 384
MODES = 720
K = 9
POLE = 4


def passed_along(value, axis, steps):
    count = lax.axis_size(axis)
    pairs = [(source, (source + steps) % count) for source in range(count)]
    return lax.ppermute(value, axis, pairs)


def extended(block, sides, width):
    for axis, dim in sides:
        count = lax.axis_size(axis)
        forward = [(i, i + 1) for i in range(count - 1)]
        forward.append((count - 1, 0))
        backward = [(target, source) for source, target in forward]
        low = lax.ppermute(
            lax.slice_in_dim(block, block.shape[dim] - width, None, axis=dim), axis, forward
        )
        high = lax.ppermute(lax.slice_in_dim(block, 0, width, axis=dim), axis, backward)
        block = jnp.concatenate([low, block, high], axis=dim)
    return block


def copy_for_each(value, axis):
    copies = jnp.broadcast_to(value, (lax.axis_size(axis), *value.shape))
    return lax.all_to_all(copies, axis, split_axis=0, concat_axis=0, tiled=True)


def joined_along(pieces, dim):
    shape = list(pieces.shape[1:])
    shape[dim] *= pieces.shape[0]
    return jnp.moveaxis(pieces, 0, dim).reshape(shape)


def collect(value, axis, dim):
    pieces = copy_for_each(value, axis)
    return joined_along(pieces, dim)


def extend(field, margin):
    cap_rows = field[:POLE]
    opposite = passed_along(cap_rows, "lon", lax.axis_size("lon") // 2)
    stacked = jnp.concatenate([opposite[::-1], field], axis=0)
    return extended(stacked, (("lon", 1),), margin)


def transform(block):
    length = block.shape[1]
    products = (
        jnp.arange(length, dtype=jnp.int32)[:, None]
        * jnp.arange(MODES, dtype=jnp.int32)[None, :]
        % length
    )
    angle = products.astype(jnp.float32) * (2.0 * math.pi / length)
    factor = 1.0 / math.sqrt(length)
    table = jnp.concatenate([jnp.cos(angle) * factor, -jnp.sin(angle) * factor], axis=1)
    table_high = table.astype(jnp.bfloat16)
    table_low = (table - table_high.astype(jnp.float32)).astype(jnp.bfloat16)
    first = jnp.einsum("rnc,nm->rcm", block, table_high, preferred_element_type=jnp.float32)
    second = jnp.einsum("rnc,nm->rcm", block, table_low, preferred_element_type=jnp.float32)
    return first + second


def shards(fields, mix_weight, basis_values, source_rows, lon_reach, quad_weights):
    lanes = basis_values.shape[2]
    margin = lanes // 2
    row_count = basis_values.shape[3]
    slab = fields.shape[0]
    own_channels = fields.shape[1] // row_count
    local = fields.reshape(slab, own_channels, row_count)
    padded = extend(local.transpose(2, 0, 1), margin)
    weight_whole = collect(mix_weight, "chan", 0)
    weight_cube = weight_whole.reshape(C, K, C)
    weight_part = lax.dynamic_slice_in_dim(
        weight_cube, lax.axis_index("chan") * own_channels, own_channels, 2
    )
    weight_used = weight_part.transpose(1, 2, 0)
    quad_ext = jnp.concatenate([quad_weights[:POLE][::-1], quad_weights], axis=0)
    row_quad = jnp.take(quad_ext, source_rows, axis=0)
    offsets = jnp.arange(lanes, dtype=jnp.int32) - margin
    keeping = jnp.abs(offsets)[None, None, :] <= lon_reach[:, :, None]
    basis_rows = basis_values.transpose(3, 0, 1, 2)
    weighted = basis_rows * row_quad[:, :, None, None]
    filters = jnp.where(keeping[:, :, None, :], weighted, jnp.zeros_like(weighted)).astype(
        jnp.bfloat16
    )
    padded_len = padded.shape[1]
    tap_ids = jnp.arange(lanes, dtype=jnp.int32)[:, None, None]
    source_ids = jnp.arange(padded_len, dtype=jnp.int32)[None, :, None]
    target_ids = jnp.arange(slab, dtype=jnp.int32)[None, None, :]
    selector = (source_ids - target_ids == tap_ids).astype(jnp.bfloat16)
    group = 4
    groups = row_count // group

    def one_group(index):
        start = index * group
        group_rows = lax.dynamic_slice_in_dim(source_rows, start, group, 0)
        group_filters = lax.dynamic_slice_in_dim(filters, start, group, 0)
        picked = jnp.take(padded, group_rows, axis=0)
        banded = jnp.einsum(
            "gekt,tpj->gekpj", group_filters, selector, preferred_element_type=jnp.float32
        ).astype(jnp.bfloat16)
        filtered = jnp.einsum(
            "gepc,gekpj->gkjc", picked, banded, preferred_element_type=jnp.float32
        ).astype(jnp.bfloat16)
        return jnp.einsum(
            "gkjc,kco->gjo", filtered, weight_used, preferred_element_type=jnp.float32
        )

    mixed_terms = lax.map(one_group, jnp.arange(groups, dtype=jnp.int32))
    mixed_terms = mixed_terms.reshape(row_count, slab, mixed_terms.shape[3])
    mixed = lax.psum_scatter(mixed_terms, "chan", scatter_dimension=2, tiled=True).astype(
        jnp.bfloat16
    )
    result = transform(lax.all_to_all(mixed, "lon", split_axis=0, concat_axis=1, tiled=True))
    return result.reshape(result.shape[0], result.shape[1] * result.shape[2])


def solution(mesh):
    placed = (P("lon", "chan"), P("chan", None), P(), P(), P(), P())
    return jax.shard_map(
        shards, mesh=mesh, in_specs=placed, out_specs=P("lon", "chan"), check_vma=False
    )
```

profile of v0, /device:TPU:103, one launch (start us, length us, event | category | flops | bytes accessed | tf_op | source)
XLA Modules:
  0.0 687.4 jit_solution(7724881797279448650)
XLA Ops:
  13.3 6.5 all-to-all-start
  20.3 4.3 gather_fusion.1
  25.5 4.0 rev.7
  39.8 6.7 copy.78
  47.5 4.2 fusion.39
  51.7 20.3 %collective-permute-done.1 = bf16[132,32,96]{2,1,0:T(8,128)(2,1)} collective-permute-done((bf16[132,32,96]{2,1,0:T(8,128)(2,1)S(1)}, bf16[132,32,96]{2,1,0:T(8,128)(2,1)}, u32[]{:S(2)}, u32[]{:S(2)}) %collective-permute-start.1) | collective-permute-done | bytes 811040 | tf_op jit(solution)/shard_map/ppermute | solution.py:26
  75.0 19.9 %collective-permute-done.2 = bf16[132,32,96]{2,1,0:T(8,128)(2,1)} collective-permute-done((bf16[132,32,96]{2,1,0:T(8,128)(2,1)}, bf16[132,32,96]{2,1,0:T(8,128)(2,1)}, u32[]{:S(2)}, u32[]{:S(2)}) %collective-permute-start.2) | collective-permute-done | bytes 811040 | tf_op jit(solution)/shard_map/ppermute | solution.py:29
  97.8 5.8 pad_maximum_fusion.1
  103.6 8.0 %copy.90 = bf16[132,109,96]{2,1,0:T(8,128)(2,1)} copy(bf16[132,109,96]{0,2,1:T(8,128)(2,1)} %pad_maximum_fusion.1) | data formatting | bytes 5524992
  111.5 5.9 copy.88
  122.1 414.6 %while.11 = (s32[]{:T(128)}, f32[32,4,45,384]{3,2,1,0:T(8,128)}, s32[32]{0:T(128)S(1)}, bf16[128,5,9,65]{3,2,1,0:T(8,128)(2,1)}, s32[128,5]{1,0:T(8,128)}, /*ind...) while((s32[]{:T(128)}, f32[32,4,45,384]{3,2,1,0:T(8,128)}, ...), condition=%wide.region_1.2_spmd.clone, body=%wide.region_0.1_spmd.clone.sunk | while | flops 405619648 | bytes 8615271 | solution.py:120
  140.1 3.9 convolution_convert_fusion.2
  208.8 4.0 fusion.70
  286.6 4.0 fusion.70
  429.1 3.9 fusion.70
  477.0 3.9 convolution_convert_fusion.2
  480.9 4.0 fusion.70
  506.8 3.9 fusion.70
  536.7 9.9 %copy.92 = f32[128,45,384]{0,1,2:T(8,128)} copy(f32[128,45,384]{2,1,0:T(8,128)} %bitcast.90) | data formatting | bytes 17694720 | tf_op jit(solution)/shard_map/reshape | solution.py:121
  546.6 84.3 %reduce-scatter.2.cloned.1.call-done = f32[128,45,96]{0,1,2:T(8,128)} async-done(((f32[128,45,384]{0,1,2:T(8,128)}), f32[128,45,96]{0,1,2:T(8,128)}) %reduce-scatter.2.cloned.1.call-update) | async-done | bytes 2211856 | tf_op jit(solution)/shard_map/reduce_scatter | solution.py:122
  635.6 7.7 %all-to-all-start.1 = ((bf16[128,45,96]{2,1,0:T(8,128)(2,1)}), bf16[128,45,96]{2,1,0:T(8,128)(2,1)S(1)}, u32[]{:S(2)}, u32[]{:S(2)}) async-start(bf16[128,45,96]{2,1,0:T(8,128)(2,1)} %copy.94), calls=%async_computation.2 | async-start | bytes 3145728 | tf_op jit(solution)/shard_map/all_to_all | solution.py:125
  643.3 19.9 %negate_multiply_fusion = (f32[1440,720]{1,0:T(8,128)}, f32[1440,720]{1,0:T(8,128)}) fusion(), kind=kLoop, calls=%fused_computation.41 | loop fusion | flops 12441600 | bytes 8294400 | tf_op jit(solution)/shard_map/mul | solution.py:66
  666.8 5.7 fusion.46
  672.5 4.6 fusion.51
  (307 shorter events, 407.0 us)
Async XLA Ops:
  6.5 5.1 copy-start.1
  8.6 11.2 %copy-start.2 = (s32[128,5]{0,1:T(8,128)S(1)}, s32[128,5]{0,1:T(8,128)}, u32[]{:S(2)}) copy-start(s32[128,5]{0,1:T(8,128)} %param.11) | copy-start | bytes 7684
  8.6 11.5 %copy-start.4 = (f32[128]{0:T(128)S(1)}, f32[128]{0:T(128)}, u32[]{:S(2)}) copy-start(f32[128]{0:T(128)} %param.13) | copy-start | bytes 1540
  8.6 16.3 %collective-permute-start = (bf16[4,45,96]{2,0,1:T(4,128)(2,1)S(1)}, bf16[4,45,96]{2,0,1:T(4,128)(2,1)S(1)}, u32[]{:S(2)}, u32[]{:S(2)}) collective-permute-start(bf16[4,45,96]{2,0,1:T(4,128)(2,1)S(1)} %copy.82), channel_id=1, source_target_pairs={{0,64},{4,68},{8,72},{12,76},{16,80},{20,84},{24,88},{28,92},{32,9... | collective-permute-start | bytes 103688 | tf_op jit(solution)/shard_map/ppermute | solution.py:17
  13.3 98.2 %all-to-all-start = ((bf16[4,96,3456]{2,1,0:T(8,128)(2,1)}), bf16[4,96,3456]{2,1,0:T(8,128)(2,1)}, u32[]{:S(2)}, u32[]{:S(2)}) async-start(bf16[4,96,3456]{2,1,0:T(8,128)(2,1)} %broadcast_in_dim.55), calls=%async_computation | async-start | bytes 5308416 | tf_op jit(solution)/shard_map/all_to_all | solution.py:36
  19.8 611.1 %reduce-scatter.2.cloned.1.call-start = ((), (), s32[]{:S(2)}) async-start(), calls=%async_computation.3 | async-start | bytes 11796480 | tf_op jit(solution)/shard_map/reduce_scatter | solution.py:122
  34.6 37.5 %collective-permute-start.1 = (bf16[132,32,96]{2,1,0:T(8,128)(2,1)S(1)}, bf16[132,32,96]{2,1,0:T(8,128)(2,1)}, u32[]{:S(2)}, u32[]{:S(2)}) collective-permute-start(bf16[132,32,96]{2,1,0:T(8,128)(2,1)S(1)} %copy.84), channel_id=1, source_target_pairs={{0,4},{4,8},{8,12},{12,16},{16,20},{20,24},{24,28},{28,32},{32,36}... | collective-permute-start | bytes 2433032 | tf_op jit(solution)/shard_map/ppermute | solution.py:26
  37.6 9.0 %copy-start.3 = (s32[128,5]{0,1:T(8,128)S(1)}, s32[128,5]{0,1:T(8,128)}, u32[]{:S(2)}) copy-start(s32[128,5]{0,1:T(8,128)} %param.12) | copy-start | bytes 7684
  37.6 57.3 %collective-permute-start.2 = (bf16[132,32,96]{2,1,0:T(8,128)(2,1)}, bf16[132,32,96]{2,1,0:T(8,128)(2,1)}, u32[]{:S(2)}, u32[]{:S(2)}) collective-permute-start(bf16[132,32,96]{2,1,0:T(8,128)(2,1)} %copy.85), channel_id=1, source_target_pairs={{4,0},{8,4},{12,8},{16,12},{20,16},{24,20},{28,24},{32,28},{36,32}... | collective-permute-start | bytes 2433032 | tf_op jit(solution)/shard_map/ppermute | solution.py:29
  635.6 27.6 %all-to-all-start.1 = ((bf16[128,45,96]{2,1,0:T(8,128)(2,1)}), bf16[128,45,96]{2,1,0:T(8,128)(2,1)S(1)}, u32[]{:S(2)}, u32[]{:S(2)}) async-start(bf16[128,45,96]{2,1,0:T(8,128)(2,1)} %copy.94), calls=%async_computation.2 | async-start | bytes 3145728 | tf_op jit(solution)/shard_map/all_to_all | solution.py:125
  664.1 8.4 %slice-start = ((s8[4423680]{0:T(1024)(128)(4,1)}), s8[229376]{0:T(1024)(128)(4,1)S(1)}, s32[]{:S(2)}) async-start(s8[4423680]{0:T(1024)(128)(4,1)} %bitcast.87), calls=%async_computation.4 | async-start | bytes 458752
  665.7 1.0 copy-start
  666.8 5.8 slice-start.1
Sparse Core Ops, SparseCore 0:
  546.7 84.1 reduce-scatter.1
where the time goes:
time: 701 us; the launch traced here: 687 us
  matrix products  262 us (37%)
  local copies, waits for them, and re-layouts  190 us (27%)
  waiting for transfers between devices  125 us (18%)
  other arithmetic  56.1 us (8%)
  loops' own time  21.5 us (3%)
  starting transfers between devices  18.7 us (3%)
  between operations  13.6 us (2%)
    dot_general x32, matrix products, one_group(): jnp.einsum('gekt,tpj->gekpj', group_filters, selector, preferred_element_...  126 us
    dot_general x32, matrix products, one_group(): jnp.einsum('gkjc,kco->gjo', filtered, weight_used, preferred_element_type...  126 us
    gather x64, local copies, waits for them, and re-layouts, one_group(): picked = jnp.take(padded, group_rows, axis=0)  97.4 us
    reduce_scatter x1, waiting for transfers between devices, shards(): lax.psum_scatter(mixed_terms, 'chan', scatter_dimension=2, tiled=True)  84.3 us
    and x32, other arithmetic, one_group(): picked = jnp.take(padded, group_rows, axis=0)  22.2 us
    another operation x1, loops' own time, shards(): mixed_terms = lax.map(one_group, jnp.arange(groups, dtype=jnp.int32))  21.5 us
    ppermute x1, waiting for transfers between devices, extended(): lax.ppermute(lax.slice_in_dim(block, block.shape[dim] - width, None, axis...  20.3 us
    ppermute x1, waiting for transfers between devices, extended(): lax.ppermute(lax.slice_in_dim(block, 0, width, axis=dim), axis, backward)  19.9 us
  transfers between devices with their start and end apart: 6, of which 3 were waited for; matrix products, arithmetic and copies ran while one was open for 10% of the time, Pallas kernels for 0%

commit v1 on v0

v1 whole, which is shorter than its diff:
```python
import functools
import math

import jax
import jax.numpy as jnp
import numpy as np
from jax import lax
from jax.experimental import pallas as pl
from jax.experimental.pallas import tpu as pltpu
from jax.sharding import Mesh, PartitionSpec as P

C = 384
MODES = 720
NLON = 1440
K = 9
NNZ = 5
POLE = 4
LINE = 8
PLANE = 16
ROWS = 16
SPAN = 24
SLAB = 45
OWN = 96
PAD = 48
WIDTH = 90
TILE = 48
EXT = 176
MESH = pl.DeviceIdType.MESH


def place():
    y, z = lax.axis_index("y"), lax.axis_index("z")
    xlo, chan = lax.axis_index("xlo"), lax.axis_index("chan")
    return y, z, xlo, chan, y * 4 + z, xlo * 4 + chan


def remote(src, dst, send, recv, where):
    return pltpu.make_async_remote_copy(
        src_ref=src, dst_ref=dst, send_sem=send, recv_sem=recv, device_id=where, device_id_type=MESH
    )


def gather_kernel(
    fields_ref, weight_ref, basis_ref, quad_ref, reach_ref,
    got_ref, halo_ref, whole_ref, filt_ref,
    wide_ref, rows_ref, tmp_ref,
    line_send, line_recv, cap_send, cap_recv, halo_send, halo_recv,
    part_send, part_recv, pair_send, pair_recv, fan_send, fan_recv, own_sem,
):
    y, z, xlo, chan, yz, me = place()
    at_line = lambda p: (y, z, p // 4, lax.rem(p, 4))
    at_plane = lambda p: (p // 4, lax.rem(p, 4), xlo, chan)
    barrier = pltpu.get_barrier_semaphore()
    for d in range(1, LINE):
        pl.semaphore_signal(barrier, inc=1, device_id=at_line(lax.rem(me + d, LINE)), device_id_type=MESH)
    for d in range(1, PLANE):
        pl.semaphore_signal(barrier, inc=1, device_id=at_plane(lax.rem(yz + d, PLANE)), device_id_type=MESH)
    pl.semaphore_wait(barrier, LINE + PLANE - 2)

    other = lax.rem(chan + 2, 4)
    twin = chan + 1 - 2 * lax.rem(chan, 2)
    far = lax.rem(twin + 2, 4)
    mine = pltpu.make_async_copy(weight_ref, whole_ref.at[chan], own_sem.at[0])
    mine.start()
    to_twin = remote(weight_ref, whole_ref.at[chan], pair_send.at[0], pair_recv.at[0], (y, z, xlo, twin))
    to_twin.start()
    piece = pl.ds(pl.multiple_of(lax.rem(yz, K) * C, 128), C)
    across = remote(
        weight_ref.at[:, piece], whole_ref.at[chan, :, piece], part_send, part_recv, (y, z, 1 - xlo, other)
    )

    @pl.when(yz < K)
    def _():
        across.start()

    shift = POLE * PAD + 3 * xlo
    zeros = jnp.zeros((128 - OWN, 128), jnp.float32)
    for l in range(SLAB):
        turned = jnp.concatenate([fields_ref[l].astype(jnp.float32), zeros], axis=0).T
        wide_ref[pl.ds(shift + l, 128, stride=PAD), :] = turned

    def narrow(row, carry):
        at = pl.multiple_of(row * PAD, PAD)
        rows_ref[row] = wide_ref[pl.ds(at, PAD), :].astype(jnp.bfloat16)
        return carry

    lax.fori_loop(POLE, POLE + 128, narrow, 0, unroll=4)
    rows_ref[POLE + 128 :] = jnp.zeros((POLE, PAD, 128), jnp.bfloat16)

    caps = [
        remote(
            rows_ref.at[POLE + g], rows_ref.at[POLE - 1 - g], cap_send.at[g], cap_recv.at[g],
            (lax.rem(y + 2, 4), z, xlo, chan),
        )
        for g in range(POLE)
    ]
    for copy in caps:
        copy.start()

    def line_copy(peer):
        span = rows_ref.at[pl.ds(pl.multiple_of(peer * ROWS, ROWS), SPAN)]
        return remote(span, got_ref.at[me], line_send.at[peer], line_recv.at[me], at_line(peer))

    for d in range(1, LINE):
        peer = lax.rem(me + d, LINE)

        @pl.when(peer != 0)
        def _():
            line_copy(peer).start()

    for copy in caps:
        copy.wait()

    @pl.when(me != 0)
    def _():
        line_copy(0).start()

    own = pltpu.make_async_copy(
        rows_ref.at[pl.ds(pl.multiple_of(me * ROWS, ROWS), SPAN)], got_ref.at[me], own_sem.at[1]
    )
    own.start()

    def fan_copy(source, target):
        part = pl.ds(pl.multiple_of(source * C, 128), C)
        return remote(
            whole_ref.at[other, :, part], whole_ref.at[other, :, part],
            fan_send.at[target], fan_recv.at[source], at_plane(target),
        )

    @pl.when(yz < K)
    def _():
        across.wait()
        for d in range(1, PLANE):
            fan_copy(yz, lax.rem(yz + d, PLANE)).start()

    def one_filter(index, carry):
        e = index // K
        k = lax.rem(index, K)
        tall = jnp.concatenate(
            [basis_ref[e, k], jnp.zeros((128 - 65, 128), jnp.float32)], axis=0
        )
        tmp_ref[...] = tall.T
        taps = tmp_ref[pl.ds(pl.multiple_of(me * ROWS, ROWS), ROWS), :]
        quads = quad_ref[e]
        reach = reach_ref[e]
        away = jnp.abs(lax.broadcasted_iota(jnp.int32, (ROWS, 128), 1) - 32)
        kept = jnp.where(away <= reach, taps * quads, 0.0)
        kept = kept.astype(jnp.bfloat16).astype(jnp.float32)
        filt_ref[pl.ds(index, ROWS, stride=TILE), :] = kept
        return carry

    lax.fori_loop(0, NNZ * K, one_filter, 0)

    def halo_copy(slot):
        side = slot // 4
        source = got_ref.at[slot, :, pl.ds(pl.multiple_of(side * 16, 16), 32)]
        target = lax.rem(yz + PLANE - 1 + 2 * side, PLANE)
        return remote(source, halo_ref.at[slot], halo_send.at[slot], halo_recv.at[slot], at_plane(target))

    own.wait()
    halo_copy(me).start()
    for d in range(1, LINE):
        slot = lax.rem(me + LINE - d, LINE)
        remote(
            rows_ref.at[pl.ds(0, SPAN)], got_ref.at[slot], line_send.at[slot], line_recv.at[slot], at_line(slot)
        ).wait_recv()
        halo_copy(slot).start()

    for source in range(K):

        @pl.when(yz != source)
        def _():
            fan_copy(source, yz).wait_recv()

    far_copy = remote(
        whole_ref.at[other], whole_ref.at[other], pair_send.at[1], pair_recv.at[1], (y, z, xlo, twin)
    )
    far_copy.start()
    for slot in range(LINE):
        halo_copy(slot).wait()
    far_copy.wait()
    to_twin.wait()
    mine.wait()
    for d in range(1, LINE):
        line_copy(lax.rem(me + d, LINE)).wait_send()

    @pl.when(yz < K)
    def _():
        for d in range(1, PLANE):
            fan_copy(yz, lax.rem(yz + d, PLANE)).wait_send()


def gather(fields, weight, basis, quads, reach):
    vmem = pl.BlockSpec(memory_space=pltpu.VMEM)
    hbm = pl.BlockSpec(memory_space=pl.ANY)
    dma = pltpu.SemaphoreType.DMA
    return pl.pallas_call(
        gather_kernel,
        out_shape=(
            jax.ShapeDtypeStruct((LINE, SPAN, PAD, 128), jnp.bfloat16),
            jax.ShapeDtypeStruct((LINE, SPAN, 32, 128), jnp.bfloat16),
            jax.ShapeDtypeStruct((4, OWN, K * C), jnp.bfloat16),
            jax.ShapeDtypeStruct((ROWS * TILE, 128), jnp.float32),
        ),
        in_specs=[vmem] * 5,
        out_specs=(hbm, hbm, hbm, vmem),
        scratch_shapes=[
            pltpu.VMEM(((128 + 2 * POLE) * PAD, 128), jnp.float32),
            pltpu.VMEM((128 + 2 * POLE, PAD, 128), jnp.bfloat16),
            pltpu.VMEM((128, 128), jnp.float32),
            dma((LINE,)), dma((LINE,)), dma((POLE,)), dma((POLE,)), dma((LINE,)), dma((LINE,)),
            dma, dma, dma((2,)), dma((2,)), dma((PLANE,)), dma((PLANE,)), dma((2,)),
        ],
        compiler_params=pltpu.CompilerParams(
            collective_id=0, has_side_effects=True, vmem_limit_bytes=48 << 20
        ),
    )(fields, weight, basis, quads, reach)


def layer_kernel(
    src_ref, filt_ref, got_ref, halo_ref, w_ref, p_ref, q_ref, u_ref, v_ref,
    out_ref,
    flat_ref, x_ref, band_ref, filtered_ref, sent_ref, all_ref, table_ref,
    send_sem, recv_sem, own_sem,
):
    y, z, xlo, chan, yz, me = place()
    source = 2 * y + z // 2
    barrier = pltpu.get_barrier_semaphore()

    def is_self(b):
        return jnp.logical_and(b == yz, source == me)

    for b in range(PLANE):

        @pl.when(jnp.logical_not(is_self(b)))
        def _():
            pl.semaphore_signal(
                barrier, inc=1, device_id=(b // 4, b % 4, source // 4, lax.rem(source, 4)), device_id_type=MESH
            )

    def lay(u, carry):
        def joined(ref, first):
            return jnp.concatenate(
                [ref[first + q, u].astype(jnp.float32)[:, :OWN] for q in range(4)], axis=1
            )

        flat_ref[0:32, :] = joined(halo_ref, 4)
        flat_ref[32:77, :] = joined(got_ref, 0)[:SLAB]
        flat_ref[77:122, :] = joined(got_ref, 4)[3:]
        flat_ref[122:154, :] = joined(halo_ref, 0)
        flat_ref[154:EXT, :] = jnp.zeros((EXT - 154, C), jnp.float32)
        x_ref[u] = flat_ref[...].astype(jnp.bfloat16)
        return carry

    lax.fori_loop(0, SPAN, lay, 0)

    targets = jnp.where(jnp.logical_and(y == me // 2, z // 2 == lax.rem(me, 2)), PLANE - 1, PLANE)
    pl.semaphore_wait(barrier, targets)

    def target_of(s):
        return me // 2, lax.rem(me, 2) * 2 + s // 2, lax.rem(s, 2)

    def send_copy(s, o):
        ty, tz, tx = target_of(s)
        return remote(
            sent_ref.at[s, o], all_ref.at[yz], send_sem.at[s, o], recv_sem.at[yz], (ty, tz, tx, o)
        )

    def own_copy(s, o):
        return pltpu.make_async_copy(sent_ref.at[s, o], all_ref.at[yz], own_sem)

    def to_self(s, o):
        ty, tz, tx = target_of(s)
        return (ty == y) & (tz == z) & (tx == xlo) & (chan == o)

    first = lax.rem(2 * z + xlo, 4)

    def one_group(step, carry):
        s = lax.rem(step + first, 4)

        def one_row(sub, carry):
            row = s * 4 + sub
            for k in range(K):
                for e in range(NNZ):
                    taps = filt_ref[pl.ds(row * TILE + e * K + k, 1), :]
                    spread = jnp.broadcast_to(taps, (TILE, 128))
                    rolled = pltpu.roll(spread, 0, 1, stride=1, stride_axis=0)
                    band_ref[pl.ds(k * TILE, TILE), pl.ds(e * 128, 128)] = rolled.astype(jnp.bfloat16)
            for half in range(2):
                window = jnp.concatenate(
                    [x_ref[src_ref[row, e], pl.ds(half * TILE, 128), :] for e in range(NNZ)], axis=0
                )
                total = jnp.dot(band_ref[...], window, preferred_element_type=jnp.float32)
                rounded = total.astype(jnp.bfloat16)
                at = pl.multiple_of(sub * (2 * TILE) + half * TILE, 16)
                for k in range(K):
                    filtered_ref[k, pl.ds(at, TILE), :] = rounded[k * TILE : (k + 1) * TILE]
            return carry

        lax.fori_loop(0, 4, one_row, 0)
        acc = jnp.zeros((4 * 2 * TILE, C), jnp.float32)
        for k in range(K):
            acc += lax.dot_general(
                filtered_ref[k],
                w_ref[:, k * C : (k + 1) * C],
                (((1,), (1,)), ((), ())),
                preferred_element_type=jnp.float32,
            )
        for o in range(4):
            piece = jnp.concatenate(
                [acc[i * 96 : (i + 1) * 96, o * OWN : (o + 1) * OWN] for i in range(4)], axis=1
            )
            sent_ref[s, o] = piece.astype(jnp.bfloat16)
        for o in range(4):

            @pl.when(to_self(s, o))
            def _():
                own_copy(s, o).start()

            @pl.when(jnp.logical_not(to_self(s, o)))
            def _():
                send_copy(s, o).start()

        return carry

    lax.fori_loop(0, 4, one_group, 0)

    def one_table(b, carry):
        at = pl.multiple_of(b * 96, 96)
        part = u_ref[pl.ds(b, 1), :] * p_ref[...] + v_ref[pl.ds(b, 1), :] * q_ref[...]
        table_ref[pl.ds(at, 96), :] = part.astype(jnp.bfloat16)
        return carry

    lax.fori_loop(0, PLANE, one_table, 0)

    for s in range(4):
        for o in range(4):

            @pl.when(to_self(s, o))
            def _():
                own_copy(s, o).wait()

            @pl.when(jnp.logical_not(to_self(s, o)))
            def _():
                send_copy(s, o).wait_send()

    for b in range(PLANE):

        @pl.when(jnp.logical_not(is_self(b)))
        def _():
            remote(
                sent_ref.at[0, 0], all_ref.at[b], send_sem.at[0, 0], recv_sem.at[b], (b // 4, b % 4, xlo, chan)
            ).wait_recv()

    block = all_ref[...].reshape(PLANE * 96, C)
    out_ref[...] = lax.dot_general(
        block, table_ref[...], (((0,), (0,)), ((), ())), preferred_element_type=jnp.float32
    )


def layer(src, filt, got, halo, weight, tables):
    vmem = pl.BlockSpec(memory_space=pltpu.VMEM)
    dma = pltpu.SemaphoreType.DMA
    return pl.pallas_call(
        layer_kernel,
        out_shape=jax.ShapeDtypeStruct((C, 2 * MODES), jnp.float32),
        in_specs=[pl.BlockSpec(memory_space=pltpu.SMEM)] + [vmem] * 8,
        out_specs=vmem,
        scratch_shapes=[
            pltpu.VMEM((EXT, C), jnp.float32),
            pltpu.VMEM((SPAN, EXT, C), jnp.bfloat16),
            pltpu.VMEM((K * TILE, NNZ * 128), jnp.bfloat16),
            pltpu.VMEM((K, 4 * 2 * TILE, C), jnp.bfloat16),
            pltpu.VMEM((4, 4, 96, C), jnp.bfloat16),
            pltpu.VMEM((PLANE, 96, C), jnp.bfloat16),
            pltpu.VMEM((PLANE * 96, 2 * MODES), jnp.bfloat16),
            dma((4, 4)), dma((PLANE,)), dma,
        ],
        compiler_params=pltpu.CompilerParams(
            collective_id=1, has_side_effects=True, vmem_limit_bytes=56 << 20
        ),
    )(src, filt, got, halo, weight, *tables)


def dft_parts():
    modes = np.arange(MODES)
    high = 2 * math.pi * ((np.arange(PLANE)[:, None] * WIDTH * modes[None]) % NLON) / NLON
    low = 2 * math.pi * ((np.arange(96)[:, None] * modes[None]) % NLON) / NLON
    factor = 1 / math.sqrt(NLON)
    inside = (np.arange(96) < WIDTH)[:, None]
    ca, sa = np.cos(high) * factor, np.sin(high) * factor
    cb, sb = np.cos(low) * inside, np.sin(low) * inside
    side = lambda a, b: jnp.asarray(np.concatenate([a, b], axis=1), jnp.float32)
    return side(cb, cb), side(sb, sb), side(ca, -sa), side(-sa, -ca)


def shards(fields, mix_weight, basis_values, source_rows, lon_reach, quad_weights):
    start = lax.axis_index(("xlo", "chan")) * ROWS
    quad_ext = jnp.concatenate([quad_weights[:POLE][::-1], quad_weights], axis=0)
    src = lax.dynamic_slice_in_dim(source_rows, start, ROWS, 0)
    reach = lax.dynamic_slice_in_dim(lon_reach, start, ROWS, 0)
    here = src[:, :, None] == jnp.arange(quad_ext.shape[0], dtype=jnp.int32)
    row_quad = jnp.sum(jnp.where(here, quad_ext, 0.0), axis=2)
    local = fields.reshape(SLAB, OWN, 128)
    got, halo, weight, filt = gather(
        local, mix_weight, basis_values, row_quad.T[:, :, None], reach.T[:, :, None]
    )
    out = layer(src - start, filt, got, halo, weight.reshape(C, K * C), dft_parts())
    return out.reshape(4, OWN * 2 * MODES)


def solution(mesh):
    fine = Mesh(mesh.devices.reshape(4, 4, 2, 4), ("y", "z", "xlo", "chan"))
    lon = ("y", "z", "xlo")
    placed = (P(lon, "chan"), P("chan", None), P(), P(), P(), P())
    return jax.shard_map(
        shards, mesh=fine, in_specs=placed, out_specs=P(lon, "chan"), check_vma=False
    )
```

time: 701 us -> 106 us (0.15)
  the two profiles are of different devices: /device:TPU:103 before, /device:TPU:7 now
where the time goes in v1:
time: 106 us
  Pallas kernels  92.6 us (87%)
  local copies, waits for them, and re-layouts  11.7 us (11%)
  other arithmetic  1.48 us (1%)
    pallas_call x1, Pallas kernels, layer(): pl.pallas_call(layer_kernel, out_shape=jax.ShapeDtypeStruct((C, 2 * MODES...  47.1 us
    pallas_call x1, Pallas kernels, gather(): pl.pallas_call(gather_kernel, out_shape=(jax.ShapeDtypeStruct((LINE, SPAN...  45.6 us
    reshape x1, local copies, waits for them, and re-layouts, shards(): return out.reshape(4, OWN * 2 * MODES)  5.01 us
    unnamed x12, local copies, waits for them, and re-layouts  4.84 us

profile of v1, /device:TPU:7, one launch (start us, length us, event | category | flops | bytes accessed | tf_op | source)
XLA Modules:
  0.0 105.9 jit_solution(2284584669934405823)
XLA Ops:
  0.0 0.0 copy-start
  0.0 0.8 rev.3
  0.8 0.7 pad_maximum_fusion
  1.5 0.0 copy-done
  1.5 0.1 constant_dynamic-slice_fusion
  1.6 0.2 select_reduce_fusion
  1.7 0.8 dynamic-slice_bitcast_fusion
  2.5 0.1 copy.21
  2.6 0.6 broadcast_subtract_fusion.src_ref
  3.2 0.1 copy.20.reach_ref
  3.3 0.1 copy.19.quad_ref
  3.4 0.0 copy-start.3
  3.4 1.5 %copy.22 = bf16[6,8,96,128]{3,2,1,0:T(8,128)(2,1)S(1)} copy(bf16[6,8,96,128]{3,1,2,0:T(8,128)(2,1)} %bitcast.14) | data formatting | bytes 2359296
  4.9 0.0 copy-start.1
  4.9 0.1 slice.4.fields_ref
  5.0 0.0 copy-done.3
  5.0 1.3 %copy-done.1 = f32[5,9,65,128]{3,2,1,0:T(8,128)S(1)} copy-done((f32[5,9,65,128]{3,2,1,0:T(8,128)S(1)}, f32[5,9,65,128]{3,2,1,0:T(8,128)}, u32[]{:S(2)}) %copy-start.1) | copy-done | bytes 1497624
  6.4 45.6 %shard_map.100 = (bf16[8,24,48,128]{3,2,1,0:T(8,128)(2,1)}, bf16[8,24,32,128]{3,2,1,0:T(8,128)(2,1)S(1)}, bf16[4,96,3456]{2,1,0:T(8,128)(2,1)}, f32[768,128]{1,0:T(8,128)S(1)}) custom-call(bf16[45,96,128]{2,1,0:T(8,128)(2,1)S(1)} %slice.4.fields_ref, bf16[96,3456]{1,0:T(8,128)(2,1)S(1)} %copy-done.3, f32[5,9,65,128]{3,2,1,0:T(8,128)S(1)} %copy-done.1, ...), custom_call_target="tpu_custom_call" | custom-call | tf_op jit(solution)/shard_map/pallas_call | solution.py:197
  51.9 0.0 copy-start.2
  51.9 1.1 %copy-done.2 = bf16[8,24,32,128]{3,2,1,0:T(8,128)(2,1)} copy-done((bf16[8,24,32,128]{3,2,1,0:T(8,128)(2,1)}, bf16[8,24,32,128]{3,2,1,0:T(8,128)(2,1)S(1)}, u32[]{:S(2)}) %copy-start.2) | copy-done | bytes 1572888
  53.1 0.0 copy-start.4
  53.1 0.7 copy-done.4
  53.8 47.1 %shard_map.101 = f32[384,1440]{1,0:T(8,128)} custom-call(s32[16,5]{1,0:T(8,128)} %broadcast_subtract_fusion.src_ref, f32[768,128]{1,0:T(8,128)} %copy-done.4, bf16[8,24,48,128]{3,2,1,0:T(8,128)(2,1)} %get-tuple-element.10.got_ref, bf16[8,24,32,128]{3,2,1,0:T(8,128)(2,1)} %copy-done.2, bf16[384,3456]{1,0:T(8,128)(2,1)} %bitcast.13, ...), custom_call_target="tpu_custom_call" | custom-call | tf_op jit(solution)/shard_map/pallas_call | solution.py:364
  100.9 5.0 %reshape.12 = f32[4,138240]{1,0:T(4,128)} reshape(f32[384,1440]{1,0:T(8,128)} %shard_map.101) | data formatting | bytes 4423680 | tf_op jit(solution)/shard_map/reshape | solution.py:409
Async XLA Ops:
  0.0 1.5 %copy-start = (s32[128,5]{0,1:T(8,128)S(1)}, s32[128,5]{0,1:T(8,128)}, u32[]{:S(2)}) copy-start(s32[128,5]{0,1:T(8,128)} %param.13) | copy-start | bytes 7684
  3.4 1.6 %copy-start.3 = (bf16[96,3456]{1,0:T(8,128)(2,1)S(1)}, bf16[96,3456]{1,0:T(8,128)(2,1)}, u32[]{:S(2)}) copy-start(bf16[96,3456]{1,0:T(8,128)(2,1)} %weight_ref.1) | copy-start | bytes 1990660
  4.9 1.4 %copy-start.1 = (f32[5,9,65,128]{3,2,1,0:T(8,128)S(1)}, f32[5,9,65,128]{3,2,1,0:T(8,128)}, u32[]{:S(2)}) copy-start(f32[5,9,65,128]{3,2,1,0:T(8,128)} %basis_ref.1) | copy-start | bytes 4492804
  51.9 1.1 %copy-start.2 = (bf16[8,24,32,128]{3,2,1,0:T(8,128)(2,1)}, bf16[8,24,32,128]{3,2,1,0:T(8,128)(2,1)S(1)}, u32[]{:S(2)}) copy-start(bf16[8,24,32,128]{3,2,1,0:T(8,128)(2,1)S(1)} %get-tuple-element.11.halo_ref) | copy-start | bytes 4718596
  53.1 0.7 copy-start.4

commit v2 on v0

v2 whole, which is shorter than its diff:
```python
import functools
import math

import jax
import jax.numpy as jnp
import numpy as np
from jax import lax
from jax.experimental import pallas as pl
from jax.experimental.pallas import tpu as pltpu
from jax.sharding import Mesh, PartitionSpec as P

C = 384
MODES = 720
NLON = 1440
K = 9
NNZ = 5
POLE = 4
LINE = 8
PLANE = 16
ROWS = 16
SPAN = 24
SLAB = 45
OWN = 96
PAD = 48
WIDTH = 90
TILE = 32
EXT = 160
TAPS = 80
PARTS = 6
MESH = pl.DeviceIdType.MESH


def place():
    y, z = lax.axis_index("y"), lax.axis_index("z")
    xlo, chan = lax.axis_index("xlo"), lax.axis_index("chan")
    return y, z, xlo, chan, y * 4 + z, xlo * 4 + chan


def remote(src, dst, send, recv, where):
    return pltpu.make_async_remote_copy(
        src_ref=src, dst_ref=dst, send_sem=send, recv_sem=recv, device_id=where, device_id_type=MESH
    )


def layer_kernel(
    src_ref, reach_ref, quad_ref, fields_ref, weight_ref, basis_in, p_in, q_in, u_in, v_in,
    out_ref,
    basis_ref, p_ref, q_ref, u_ref, v_ref, load_sem,
    tall_ref, wide_ref, rows_ref, tmp_ref, got_ref, edge_ref, halo_ref, land_ref, whole_ref, filt_ref, flat_ref, x_ref,
    even_ref, odd_ref, filtered_ref, sent_ref, all_ref, table_ref, result_ref,
    line_send, line_recv, cap_send, cap_recv, halo_send, halo_recv,
    part_send, part_recv, pair_send, pair_recv, fan_z_send, fan_z_recv, fan_y_send, fan_y_recv, own_sem,
    send_sem, recv_sem, ready_sem, stage_ref, out_sem,
):
    y, z, xlo, chan, yz, me = place()
    at_line = lambda p: (y, z, p // 4, lax.rem(p, 4))
    at_plane = lambda p: (p // 4, lax.rem(p, 4), xlo, chan)
    source = 2 * y + z // 2
    barrier = pltpu.get_barrier_semaphore()

    def signal(where):
        pl.semaphore_signal(barrier, inc=1, device_id=where, device_id_type=MESH)

    for d in range(1, LINE):
        signal(at_line(lax.rem(me + d, LINE)))
    for d in range(1, PLANE):
        signal(at_plane(lax.rem(yz + d, PLANE)))
    loads = [
        pltpu.make_async_copy(a, b, load_sem.at[i])
        for i, (a, b) in enumerate(
            [(basis_in, basis_ref), (p_in, p_ref), (q_in, q_ref), (u_in, u_ref), (v_in, v_ref)]
        )
    ]
    for copy in loads:
        copy.start()

    for c in range(OWN):
        tall_ref[c * PAD : c * PAD + SLAB, :] = fields_ref[:, c * 128 : (c + 1) * 128].astype(jnp.float32)
    shift = POLE * PAD + 3 * xlo
    zeros = jnp.zeros((128 - OWN, 128), jnp.float32)
    for l in range(SLAB):
        turned = jnp.concatenate([tall_ref[pl.ds(l, OWN, stride=PAD), :], zeros], axis=0).T
        wide_ref[pl.ds(shift + l, 128, stride=PAD), :] = turned

    def narrow(row, carry):
        at = pl.multiple_of(row * PAD, PAD)
        rows_ref[row] = wide_ref[pl.ds(at, PAD), :].astype(jnp.bfloat16)
        return carry

    lax.fori_loop(POLE, POLE + 128, narrow, 0, unroll=4)
    rows_ref[POLE + 128 :] = jnp.zeros((POLE, PAD, 128), jnp.bfloat16)

    pl.semaphore_wait(barrier, LINE + PLANE - 2)
    for d in range(1, LINE):
        pl.semaphore_signal(
            ready_sem, inc=1, device_id=at_line(lax.rem(me + d, LINE)), device_id_type=MESH
        )

    caps = [
        remote(
            rows_ref.at[POLE + g], rows_ref.at[POLE - 1 - g], cap_send.at[g], cap_recv.at[g],
            (lax.rem(y + 2, 4), z, xlo, chan),
        )
        for g in range(POLE)
    ]
    for copy in caps:
        copy.start()

    other = lax.rem(chan + 2, 4)
    twin = chan + 1 - 2 * lax.rem(chan, 2)
    part_spot = lambda p: pl.ds(pl.multiple_of(p * C, 128), C)
    owned = y + 4 * z
    piece = part_spot(lax.rem(owned, K))
    across = remote(
        weight_ref.at[:, piece], whole_ref.at[chan, :, piece], part_send, part_recv, (y, z, 1 - xlo, other)
    )

    @pl.when(owned < K)
    def _():
        across.start()

    def line_copy(peer, c):
        return remote(
            rows_ref.at[pl.ds(peer * ROWS + 4 * c, 4)], got_ref.at[me, pl.ds(4 * c, 4)],
            line_send.at[peer, c], line_recv.at[me, c], at_line(peer),
        )

    def takes(peer, c):
        return lax.rem(peer, 2) * 2 + 4 > c

    def each_line(c, act):
        for d in range(1, LINE):
            peer = lax.rem(me + d, LINE)
            if isinstance(c, int) and c < 4:
                act(peer)
            else:
                pl.when(takes(peer, c))(functools.partial(act, peer))

    for d in range(1, LINE):
        peer = lax.rem(me + d, LINE)

        @pl.when(peer != 0)
        def _():
            line_copy(peer, 0).start()

    each_line(1, lambda peer: line_copy(peer, 1).start())

    def advance(c):
        each_line(c - 2, lambda peer: line_copy(peer, c - 2).wait_send())
        each_line(c, lambda peer: line_copy(peer, c).start())

    mine = pltpu.make_async_copy(weight_ref, whole_ref.at[chan], own_sem.at[0])
    mine.start()
    to_twin = remote(weight_ref, whole_ref.at[chan], pair_send.at[0], pair_recv.at[0], (y, z, xlo, twin))
    to_twin.start()

    for copy in caps:
        copy.wait()

    @pl.when(me != 0)
    def _():
        line_copy(0, 0).start()

    own = pltpu.make_async_copy(
        rows_ref.at[pl.ds(me * ROWS, SPAN)], got_ref.at[me], own_sem.at[1]
    )
    own.start()
    for copy in loads:
        copy.wait()

    def one_filter(k, carry):
        for e in range(NNZ):
            tall = jnp.concatenate(
                [basis_ref[e, k], jnp.zeros((128 - 65, 128), jnp.float32)], axis=0
            )
            tmp_ref[e] = tall.T
        for e in range(NNZ):
            taps = tmp_ref[e, pl.ds(pl.multiple_of(me * ROWS, ROWS), ROWS), :]
            filt_ref[pl.ds(e * 16 + k, ROWS, stride=TAPS), :] = taps
        return carry

    lax.fori_loop(0, K, one_filter, 0)
    away = jnp.abs(lax.broadcasted_iota(jnp.int32, (16, 128), 1) - 32)

    def scale(row, carry):
        for e in range(NNZ):
            from_row = src_ref[e, me * ROWS + row]
            quad = quad_ref[jnp.where(from_row < POLE, POLE - 1 - from_row, from_row - POLE)]
            reach = reach_ref[e, me * ROWS + row]
            at = pl.ds(pl.multiple_of(row * TAPS + e * 16, 16), 16)
            kept = jnp.where(away <= reach, filt_ref[at, :] * quad, 0.0)
            filt_ref[at, :] = kept.astype(jnp.bfloat16).astype(jnp.float32)
        return carry

    lax.fori_loop(0, ROWS, scale, 0)

    def fan_z(target):
        return remote(
            whole_ref.at[other, :, piece], whole_ref.at[other, :, piece],
            fan_z_send.at[target], fan_z_recv.at[z], (y, target, xlo, chan),
        )

    @pl.when(owned < K)
    def _():
        across.wait()
        for d in range(1, 4):
            fan_z(lax.rem(z + d, 4)).start()

    advance(2)

    def fan_y(j, target):
        at = whole_ref.at[other, :, part_spot(y + 4 * j)]
        return remote(at, at, fan_y_send.at[j, target], fan_y_recv.at[y, j], (target, z, xlo, chan))

    def fan_y_from(start, j):
        at = whole_ref.at[other, :, start * C + 4 * j * C : start * C + 4 * j * C + C]
        return remote(at, at, fan_y_send.at[j, start], fan_y_recv.at[start, j], (start, z, xlo, chan))

    def each_piece(act):
        for j in range(3):
            if j < 2:
                act(j)
            else:
                pl.when(y == 0)(functools.partial(act, j))

    def pass_on(j):
        at = whole_ref.at[other, :, part_spot(y + 4 * j)]

        @pl.when(z != j)
        def _():
            remote(at, at, fan_z_send.at[0], fan_z_recv.at[j], (y, j, xlo, chan)).wait_recv()

        for d in range(1, 4):
            fan_y(j, lax.rem(y + d, 4)).start()

    each_piece(pass_on)
    advance(3)

    def one_table(b, carry):
        at = pl.multiple_of(b * 96, 96)
        part = u_ref[pl.ds(b, 1), :] * p_ref[...] + v_ref[pl.ds(b, 1), :] * q_ref[...]
        table_ref[pl.ds(at, 96), :] = part.astype(jnp.bfloat16)
        return carry

    lax.fori_loop(0, PLANE, one_table, 0)


    def halo_copy(side, c):
        target = lax.rem(yz + PLANE - 1 + 2 * side, PLANE)
        return remote(
            edge_ref.at[side, pl.ds(4 * c, 4)], halo_ref.at[side, pl.ds(4 * c, 4)],
            halo_send.at[side, c], halo_recv.at[side, c], at_plane(target),
        )

    def joined(first, u):
        return jnp.concatenate(
            [got_ref[first + q, u].astype(jnp.float32)[:, :OWN] for q in range(4)], axis=1
        )

    def arrive(c):
        for d in range(1, LINE):
            slot = lax.rem(me + LINE - d, LINE)
            remote(
                rows_ref.at[pl.ds(0, 4)], got_ref.at[slot, pl.ds(4 * c, 4)],
                line_send.at[slot, c], line_recv.at[slot, c], at_line(slot),
            ).wait_recv()

        def one(i, carry):
            u = 4 * c + i
            left, right = joined(0, u), joined(4, u)
            edge_ref[0, u] = left[:32].astype(jnp.bfloat16)
            edge_ref[1, u] = right[16:].astype(jnp.bfloat16)
            flat_ref[u, 32:77, :] = left[:SLAB]
            flat_ref[u, 77:122, :] = right[3:]
            return carry

        lax.fori_loop(0, 4, one, 0)
        for side in range(2):
            halo_copy(side, c).start()

    def finish(c):
        for side in range(2):
            halo_copy(side, c).wait_recv()

        def one(i, carry):
            u = 4 * c + i
            flat_ref[u, 0:32, :] = halo_ref[1, u].astype(jnp.float32)
            flat_ref[u, 122:154, :] = halo_ref[0, u].astype(jnp.float32)
            flat_ref[u, 154:EXT, :] = jnp.zeros((EXT - 154, C), jnp.float32)
            x_ref[u] = flat_ref[u].astype(jnp.bfloat16)
            return carry

        lax.fori_loop(0, 4, one, 0)

    odd = lax.rem(me, 2) == 1
    twin_copy = remote(
        x_ref.at[pl.ds(0, 8)], land_ref, pair_send.at[2], pair_recv.at[2], (y, z, xlo, twin)
    )

    def late(c):
        @pl.when(odd)
        def _():
            finish(c)

        @pl.when(jnp.logical_not(odd) & (c == 4))
        def _():
            twin_copy.wait_recv()

        @pl.when(jnp.logical_not(odd))
        def _():
            def one(i, carry):
                x_ref[4 * c + i] = land_ref[4 * c - 16 + i]
                return carry

            lax.fori_loop(0, 4, one, 0)

    far_copy = remote(
        whole_ref.at[other], whole_ref.at[other], pair_send.at[1], pair_recv.at[1], (y, z, xlo, twin)
    )
    own.wait()
    arrive(0)
    advance(4)
    arrive(1)
    arrive(2)
    advance(5)
    for start in range(4):
        for j in range(3 if start == 0 else 2):

            @pl.when(y != start)
            def _():
                fan_y_from(start, j).wait_recv()

    far_copy.start()
    for c in range(3):
        finish(c)

    @pl.when(odd)
    def _():
        twin_copy.start()

    lane = lax.broadcasted_iota(jnp.int32, (TILE, 128), 1)

    def build(row, band_ref):
        for k in range(K):
            turned = []
            for e in range(NNZ):
                taps = filt_ref[pl.ds(row * TAPS + e * 16 + k, 1), :]
                spread = jnp.broadcast_to(taps, (TILE, 128))
                turned.append(pltpu.roll(spread, 96 * e % 128, 1, stride=1, stride_axis=0))
            tiles = [
                jnp.where(lane < 96, turned[0], turned[1]),
                jnp.where(lane < 64, turned[1], turned[2]),
                jnp.where(lane < 32, turned[2], turned[3]),
                turned[4],
            ]
            for t in range(4):
                band_ref[k * TILE : (k + 1) * TILE, t * 128 : (t + 1) * 128] = tiles[t].astype(jnp.bfloat16)

    def convolve(row, band_ref):
        sources = [jnp.clip(src_ref[e, me * ROWS + row] - me * ROWS, 0, SPAN - 1) for e in range(NNZ)]
        windows = []
        for b in range(3):
            pieces = [x_ref[u, b * TILE : b * TILE + 96, :] for u in sources]
            windows.append(jnp.concatenate(pieces + [x_ref[sources[0], 0:32, :]], axis=0))
        total = jnp.dot(
            band_ref[...], jnp.concatenate(windows, axis=1), preferred_element_type=jnp.float32
        )
        rounded = total.astype(jnp.bfloat16)
        for b in range(3):
            at = pl.multiple_of(lax.rem(row, 4) * 96 + b * TILE, TILE)
            for k in range(K):
                filtered_ref[pl.ds(at, TILE), k * C : (k + 1) * C] = rounded[
                    k * TILE : (k + 1) * TILE, b * C : (b + 1) * C
                ]

    ty, tz = me // 2, lax.rem(me, 2) * 2

    def to_self(s, o):
        return (ty == y) & (tz + s // 2 == z) & (lax.rem(s, 2) == xlo) & (chan == o)

    def send_copy(s, o):
        return remote(
            sent_ref.at[s, o], all_ref.at[yz], send_sem.at[s, o], recv_sem.at[yz],
            (ty, tz + s // 2, lax.rem(s, 2), o),
        )

    def own_copy(s, o):
        return pltpu.make_async_copy(sent_ref.at[s, o], all_ref.at[yz], own_sem.at[2])

    build(0, even_ref)

    def pair(p, carry):
        c = p // 2

        @pl.when(p == 2)
        def _():
            finish(3)

        @pl.when((lax.rem(p, 2) == 0) & (p > 2))
        def _():
            late(c + 2)

        convolve(2 * p, even_ref)
        build(2 * p + 1, odd_ref)
        convolve(2 * p + 1, odd_ref)
        build(jnp.minimum(2 * p + 2, ROWS - 1), even_ref)

        @pl.when((p == 0) | ((p < 3) & odd))
        def _():
            arrive(p + 3)

        @pl.when(p == 1)
        def _():
            far_copy.wait()
            to_twin.wait()
            pl.semaphore_wait(ready_sem, LINE - 1)
            mine.wait()

        @pl.when(lax.rem(p, 2) == 1)
        def _():
            acc = lax.dot_general(
                filtered_ref[...],
                whole_ref[...].reshape(C, K * C),
                (((1,), (1,)), ((), ())),
                preferred_element_type=jnp.float32,
            )
            for o in range(4):
                joint = jnp.concatenate(
                    [acc[i * 96 : (i + 1) * 96, o * OWN : (o + 1) * OWN] for i in range(4)], axis=1
                )
                sent_ref[c, o] = joint.astype(jnp.bfloat16)
            for o in range(4):

                @pl.when(to_self(c, o))
                def _():
                    own_copy(c, o).start()

                @pl.when(jnp.logical_not(to_self(c, o)))
                def _():
                    send_copy(c, o).start()

        return carry

    lax.fori_loop(0, 8, pair, 0)

    for s in range(4):
        for o in range(4):

            @pl.when(to_self(s, o))
            def _():
                own_copy(s, o).wait()

            @pl.when(jnp.logical_not(to_self(s, o)))
            def _():
                send_copy(s, o).wait_send()

    for c in range(PARTS):

        def edges_left(c=c):
            for side in range(2):
                halo_copy(side, c).wait_send()

        if c < 4:
            edges_left()
        else:
            pl.when(odd)(edges_left)
        if c >= 4:
            each_line(c, lambda peer: line_copy(peer, c).wait_send())

    @pl.when(odd)
    def _():
        twin_copy.wait_send()

    @pl.when(owned < K)
    def _():
        for d in range(1, 4):
            fan_z(lax.rem(z + d, 4)).wait_send()

    def left(j):
        for d in range(1, 4):
            fan_y(j, lax.rem(y + d, 4)).wait_send()

    each_piece(left)

    for b in range(PLANE):

        @pl.when(jnp.logical_not(jnp.logical_and(b == yz, source == me)))
        def _():
            remote(
                sent_ref.at[0, 0], all_ref.at[b], send_sem.at[0, 0], recv_sem.at[b], (b // 4, b % 4, xlo, chan)
            ).wait_recv()

    result = lax.dot_general(
        all_ref[...].reshape(PLANE * 96, C),
        table_ref[...],
        (((0,), (0,)), ((), ())),
        preferred_element_type=jnp.float32,
    )
    for t in range(12):
        result_ref[t * C : (t + 1) * C, :] = result[:, 128 * t : 128 * (t + 1)]

    def out_copy(g):
        at = pl.ds(45 * g, 45)
        return pltpu.make_async_copy(stage_ref.at[at], out_ref.at[at], out_sem.at[g])

    def store(g, carry):
        pieces = []
        for j in range(4):
            tiles = [result_ref[pl.ds(t * C + 4 * g + j, 4, stride=OWN), :] for t in range(12)]
            pieces += tiles[:11] + [tiles[11][:, :32]]
        four = jnp.concatenate(pieces, axis=1)
        for t in range(45):
            stage_ref[45 * g + t] = four[:, 128 * t : 128 * (t + 1)]
        out_copy(g).start()
        return carry

    lax.fori_loop(0, OWN // 4, store, 0)
    for g in range(OWN // 4):
        out_copy(g).wait()


def layer(src, reach, quads, fields, weight, basis, tables):
    vmem = pl.BlockSpec(memory_space=pltpu.VMEM)
    smem = pl.BlockSpec(memory_space=pltpu.SMEM)
    dma = pltpu.SemaphoreType.DMA
    wide = 128 + 2 * POLE
    bf16 = jnp.bfloat16
    return pl.pallas_call(
        layer_kernel,
        out_shape=jax.ShapeDtypeStruct((OWN * 2 * MODES // 128, 4, 128), jnp.float32),
        in_specs=[smem] * 3 + [vmem] * 2 + [pl.BlockSpec(memory_space=pl.ANY)] * 5,
        out_specs=pl.BlockSpec(memory_space=pl.ANY),
        scratch_shapes=[
            *[pltpu.VMEM(a.shape, a.dtype) for a in (basis, *tables)],
            dma((5,)),
            pltpu.VMEM((OWN * PAD, 128), jnp.float32),
            pltpu.VMEM((wide * PAD, 128), jnp.float32),
            pltpu.VMEM((wide, PAD, 128), bf16),
            pltpu.VMEM((NNZ, 128, 128), jnp.float32),
            pltpu.VMEM((LINE, SPAN, PAD, 128), bf16),
            pltpu.VMEM((2, SPAN, 32, C), bf16),
            pltpu.VMEM((2, SPAN, 32, C), bf16),
            pltpu.VMEM((8, EXT, C), bf16),
            pltpu.VMEM((4, OWN, K * C), bf16),
            pltpu.VMEM((ROWS * TAPS, 128), jnp.float32),
            pltpu.VMEM((SPAN, EXT, C), jnp.float32),
            pltpu.VMEM((SPAN, EXT, C), bf16),
            pltpu.VMEM((K * TILE, 512), bf16),
            pltpu.VMEM((K * TILE, 512), bf16),
            pltpu.VMEM((4 * 96, K * C), bf16),
            pltpu.VMEM((4, 4, 96, C), bf16),
            pltpu.VMEM((PLANE, 96, C), bf16),
            pltpu.VMEM((PLANE * 96, 1536), bf16),
            pltpu.VMEM((12 * C, 128), jnp.float32),
            dma((LINE, PARTS)), dma((LINE, PARTS)), dma((POLE,)), dma((POLE,)), dma((2, PARTS)), dma((2, PARTS)),
            dma, dma, dma((3,)), dma((3,)), dma((4,)), dma((4,)), dma((3, 4)), dma((4, 3)), dma((3,)),
            dma((4, 4)), dma((PLANE,)), pltpu.SemaphoreType.REGULAR,
            pltpu.VMEM((OWN * 2 * MODES // 128, 4, 128), jnp.float32), dma((OWN // 4,)),
        ],
        compiler_params=pltpu.CompilerParams(
            collective_id=0, has_side_effects=True, vmem_limit_bytes=60 << 20
        ),
    )(src, reach, quads, fields, weight, basis, *tables)


def dft_parts():
    modes = np.arange(MODES)
    high = 2 * math.pi * ((np.arange(PLANE)[:, None] * WIDTH * modes[None]) % NLON) / NLON
    low = 2 * math.pi * ((np.arange(96)[:, None] * modes[None]) % NLON) / NLON
    factor = 1 / math.sqrt(NLON)
    inside = (np.arange(96) < WIDTH)[:, None]
    ca, sa = np.cos(high) * factor, np.sin(high) * factor
    cb, sb = np.cos(low) * inside, np.sin(low) * inside
    side = lambda a, b: jnp.asarray(np.concatenate([a, b, 0 * a[:, :96]], axis=1), jnp.float32)
    return side(cb, cb), side(sb, sb), side(ca, -sa), side(-sa, -ca)


def shards(fields, mix_weight, basis_values, source_rows, lon_reach, quad_weights):
    out = layer(
        source_rows.T, lon_reach.T, quad_weights, fields, mix_weight, basis_values, dft_parts()
    )
    return out.transpose(1, 0, 2).reshape(4, OWN * 2 * MODES)


def solution(mesh):
    fine = Mesh(mesh.devices.reshape(4, 4, 2, 4), ("y", "z", "xlo", "chan"))
    lon = ("y", "z", "xlo")
    placed = (P(lon, "chan"), P("chan", None), P(), P(), P(), P())
    return jax.shard_map(
        shards, mesh=fine, in_specs=placed, out_specs=P(lon, "chan"), check_vma=False
    )
```

time: 701 us -> 77.8 us (0.11); the launches traced: 687 us -> 77 us
  matrix products: 262 us -> 0 us
  local copies, waits for them, and re-layouts: 190 us -> 2.68 us
  waiting for transfers between devices: 125 us -> 0 us
  Pallas kernels: 0 us -> 74.3 us
  other arithmetic: 56.1 us -> 0 us
  loops' own time: 21.5 us -> 0 us
  starting transfers between devices: 18.7 us -> 0 us
  between operations: 13.6 us -> 0.01 us
    dot_general x66 -> x0, matrix products: 262 us -> none  [the longest x32 126 us: one_group(): jnp.einsum('gekt,tpj->gekpj', group_filters, selector, preferred_element_...]
    gather x67 -> x0, local copies, waits for them, and re-layouts: 102 us -> none  [the longest x64 97.4 us: one_group(): picked = jnp.take(padded, group_rows, axis=0)]
    reduce_scatter x1 -> x0, waiting for transfers between devices: 84.3 us -> none  [shards(): lax.psum_scatter(mixed_terms, 'chan', scatter_dimension=2, tiled=True)]
    pallas_call x0 -> x1, Pallas kernels: none -> 74.3 us  [layer(): pl.pallas_call(layer_kernel, out_shape=jax.ShapeDtypeStruct((OWN * 2 * MO...]
    ppermute x3 -> x0, waiting for transfers between devices: 40.2 us -> none  [the longest x1 20.3 us: extended(): lax.ppermute(lax.slice_in_dim(block, block.shape[dim] - width, None, axis...]
    and x32 -> x0, other arithmetic: 22.2 us -> none  [one_group(): picked = jnp.take(padded, group_rows, axis=0)]
    another operation x1 -> x0, loops' own time: 21.5 us -> none  [shards(): mixed_terms = lax.map(one_group, jnp.arange(groups, dtype=jnp.int32))]
    mul x1 -> x0, other arithmetic: 19.9 us -> none  [transform(): -jnp.sin(angle) * factor]
  transfers between devices with their start and end apart: 6 -> 0, of which waited for: 3 -> 0; matrix products, arithmetic and copies ran while one was open for 10% -> 0% of each run, Pallas kernels for 0% -> 0%
where the time goes in v2:
time: 77.8 us; the launch traced here: 77 us
  Pallas kernels  74.3 us (96%)
  local copies, waits for them, and re-layouts  2.68 us (3%)
    pallas_call x1, Pallas kernels, layer(): pl.pallas_call(layer_kernel, out_shape=jax.ShapeDtypeStruct((OWN * 2 * MO...  74.3 us
    unnamed x1, local copies, waits for them, and re-layouts  2.68 us

profile of v2, /device:TPU:103, one launch (start us, length us, event | category | flops | bytes accessed | tf_op | source)
XLA Modules:
  0.0 77.0 jit_solution(15439343349603371825)
XLA Ops:
  0.0 74.3 %shard_map.100 = f32[1080,4,128]{2,1,0:T(4,128)} custom-call(s32[5,128]{1,0:T(8,128)} %bitcast.6, s32[5,128]{1,0:T(8,128)} %bitcast.7, f32[128]{0:T(128)} %quad_ref.1, bf16[45,12288]{1,0:T(8,128)(2,1)} %fields_ref.1, bf16[96,3456]{1,0:T(8,128)(2,1)} %weight_ref.1, f32[5,9,65,128]{3,2,1,0:T(8,128)} %basis_in.1, f32[96,1536]{1,0:T(8,128)} %constant.8.clone.p_in, ...), custom_call_target="tpu_custom_call" | custom-call | tf_op jit(solution)/shard_map/pallas_call | solution.py:528
  74.3 2.7 %copy.12 = f32[4,138240]{1,0:T(4,128)} copy(f32[4,138240]{1,0:T(4,128)} %bitcast.5) | data formatting | bytes 4423680

commit v3 on v2

--- a/solution.py
+++ b/solution.py
@@ -292,7 +292,6 @@
 
         lax.fori_loop(0, 4, one, 0)
 
-    odd = lax.rem(me, 2) == 1
     twin_copy = remote(
         x_ref.at[pl.ds(0, 8)], land_ref, pair_send.at[2], pair_recv.at[2], (y, z, xlo, twin)
     )
@@ -317,12 +316,19 @@
     far_copy = remote(
         whole_ref.at[other], whole_ref.at[other], pair_send.at[1], pair_recv.at[1], (y, z, xlo, twin)
     )
+    odd = lax.rem(me, 2) == 1
     own.wait()
     arrive(0)
     advance(4)
     arrive(1)
     arrive(2)
     advance(5)
+    arrive(3)
+
+    @pl.when(odd)
+    def _():
+        arrive(4)
+
     for start in range(4):
         for j in range(3 if start == 0 else 2):
 
@@ -405,9 +411,9 @@
         convolve(2 * p + 1, odd_ref)
         build(jnp.minimum(2 * p + 2, ROWS - 1), even_ref)
 
-        @pl.when((p == 0) | ((p < 3) & odd))
-        def _():
-            arrive(p + 3)
+        @pl.when((p == 0) & odd)
+        def _():
+            arrive(5)
 
         @pl.when(p == 1)
         def _():
@@ -504,18 +510,23 @@
         return pltpu.make_async_copy(stage_ref.at[at], out_ref.at[at], out_sem.at[g])
 
     def store(g, carry):
-        pieces = []
-        for j in range(4):
-            tiles = [result_ref[pl.ds(t * C + 4 * g + j, 4, stride=OWN), :] for t in range(12)]
-            pieces += tiles[:11] + [tiles[11][:, :32]]
-        four = jnp.concatenate(pieces, axis=1)
+        tiles = []
+        for j in range(8):
+            tiles.append([result_ref[pl.ds(t * C + 8 * g + j, 4, stride=OWN), :] for t in range(12)])
+        flat = []
+        for half in range(2):
+            pieces = []
+            for j in range(4):
+                pieces += tiles[4 * half + j][:11] + [tiles[4 * half + j][11][:, :32]]
+            four = jnp.concatenate(pieces, axis=1)
+            flat += [four[:, 128 * t : 128 * (t + 1)] for t in range(45)]
         for t in range(45):
-            stage_ref[45 * g + t] = four[:, 128 * t : 128 * (t + 1)]
+            stage_ref[45 * g + t] = jnp.concatenate(flat[2 * t : 2 * t + 2], axis=0)
         out_copy(g).start()
         return carry
 
-    lax.fori_loop(0, OWN // 4, store, 0)
-    for g in range(OWN // 4):
+    lax.fori_loop(0, OWN // 8, store, 0)
+    for g in range(OWN // 8):
         out_copy(g).wait()
 
 
@@ -527,7 +538,7 @@
     bf16 = jnp.bfloat16
     return pl.pallas_call(
         layer_kernel,
-        out_shape=jax.ShapeDtypeStruct((OWN * 2 * MODES // 128, 4, 128), jnp.float32),
+        out_shape=jax.ShapeDtypeStruct((OWN * MODES // 128, 8, 128), jnp.float32),
         in_specs=[smem] * 3 + [vmem] * 2 + [pl.BlockSpec(memory_space=pl.ANY)] * 5,
         out_specs=pl.BlockSpec(memory_space=pl.ANY),
         scratch_shapes=[
@@ -555,7 +566,7 @@
             dma((LINE, PARTS)), dma((LINE, PARTS)), dma((POLE,)), dma((POLE,)), dma((2, PARTS)), dma((2, PARTS)),
             dma, dma, dma((3,)), dma((3,)), dma((4,)), dma((4,)), dma((3, 4)), dma((4, 3)), dma((3,)),
             dma((4, 4)), dma((PLANE,)), pltpu.SemaphoreType.REGULAR,
-            pltpu.VMEM((OWN * 2 * MODES // 128, 4, 128), jnp.float32), dma((OWN // 4,)),
+            pltpu.VMEM((OWN * MODES // 128, 8, 128), jnp.float32), dma((OWN // 8,)),
         ],
         compiler_params=pltpu.CompilerParams(
             collective_id=0, has_side_effects=True, vmem_limit_bytes=60 << 20
@@ -579,6 +590,7 @@
     out = layer(
         source_rows.T, lon_reach.T, quad_weights, fields, mix_weight, basis_values, dft_parts()
     )
+    out = out.reshape(OWN * 2 * MODES // 128, 4, 128)
     return out.transpose(1, 0, 2).reshape(4, OWN * 2 * MODES)
 
 

time: 77.8 us -> 72.3 us (0.929)
  Pallas kernels: 74.3 us -> 69.5 us
    pallas_call x1, Pallas kernels: 74.3 us -> 69.5 us  [layer(): pl.pallas_call(layer_kernel, out_shape=jax.ShapeDtypeStruct((OWN * MODES...]
where the time goes in v3:
time: 72.3 us; the launch traced here: 72.2 us
  Pallas kernels  69.5 us (96%)
  local copies, waits for them, and re-layouts  2.68 us (4%)
    pallas_call x1, Pallas kernels, layer(): pl.pallas_call(layer_kernel, out_shape=jax.ShapeDtypeStruct((OWN * MODES...  69.5 us
    unnamed x1, local copies, waits for them, and re-layouts  2.68 us

profile of v3, /device:TPU:103, one launch (start us, length us, event | category | flops | bytes accessed | tf_op | source)
XLA Modules:
  0.0 72.2 jit_solution(16116391273983452460)
XLA Ops:
  0.0 69.5 %shard_map.100 = f32[540,8,128]{2,1,0:T(8,128)} custom-call(s32[5,128]{1,0:T(8,128)} %bitcast.8, s32[5,128]{1,0:T(8,128)} %bitcast.9, f32[128]{0:T(128)} %quad_ref.1, bf16[45,12288]{1,0:T(8,128)(2,1)} %fields_ref.1, bf16[96,3456]{1,0:T(8,128)(2,1)} %weight_ref.1, f32[5,9,65,128]{3,2,1,0:T(8,128)} %basis_in.1, f32[96,1536]{1,0:T(8,128)} %constant.8.clone.p_in, ...), custom_call_target="tpu_custom_call" | custom-call | tf_op jit(solution)/shard_map/pallas_call | solution.py:539
  69.5 2.7 %copy.13 = f32[4,138240]{1,0:T(4,128)} copy(f32[4,138240]{1,0:T(4,128)} %bitcast.7) | data formatting | bytes 4423680

commit v4 on v3

--- a/solution.py
+++ b/solution.py
@@ -122,8 +122,12 @@
     def line_copy(peer, c):
         return remote(
             rows_ref.at[pl.ds(peer * ROWS + 4 * c, 4)], got_ref.at[me, pl.ds(4 * c, 4)],
-            line_send.at[peer, c], line_recv.at[me, c], at_line(peer),
-        )
+            line_send.at[c], line_recv.at[c], at_line(peer),
+        )
+
+    def line_all(c, count):
+        both = got_ref.at[pl.ds(0, count), pl.ds(0, 4)]
+        return remote(both, both, line_send.at[c], line_recv.at[c], at_line(lax.rem(me + 1, LINE)))
 
     def takes(peer, c):
         return lax.rem(peer, 2) * 2 + 4 > c
@@ -146,7 +150,7 @@
     each_line(1, lambda peer: line_copy(peer, 1).start())
 
     def advance(c):
-        each_line(c - 2, lambda peer: line_copy(peer, c - 2).wait_send())
+        line_all(c - 2, LINE - 1).wait_send()
         each_line(c, lambda peer: line_copy(peer, c).start())
 
     mine = pltpu.make_async_copy(weight_ref, whole_ref.at[chan], own_sem.at[0])
@@ -249,8 +253,12 @@
         target = lax.rem(yz + PLANE - 1 + 2 * side, PLANE)
         return remote(
             edge_ref.at[side, pl.ds(4 * c, 4)], halo_ref.at[side, pl.ds(4 * c, 4)],
-            halo_send.at[side, c], halo_recv.at[side, c], at_plane(target),
-        )
+            halo_send.at[c], halo_recv.at[c], at_plane(target),
+        )
+
+    def halo_both(c):
+        both = halo_ref.at[:, pl.ds(0, 4)]
+        return remote(both, both, halo_send.at[c], halo_recv.at[c], at_plane(lax.rem(yz + 1, PLANE)))
 
     def joined(first, u):
         return jnp.concatenate(
@@ -258,12 +266,7 @@
         )
 
     def arrive(c):
-        for d in range(1, LINE):
-            slot = lax.rem(me + LINE - d, LINE)
-            remote(
-                rows_ref.at[pl.ds(0, 4)], got_ref.at[slot, pl.ds(4 * c, 4)],
-                line_send.at[slot, c], line_recv.at[slot, c], at_line(slot),
-            ).wait_recv()
+        line_all(c, LINE - 1).wait_recv()
 
         def one(i, carry):
             u = 4 * c + i
@@ -279,8 +282,7 @@
             halo_copy(side, c).start()
 
     def finish(c):
-        for side in range(2):
-            halo_copy(side, c).wait_recv()
+        halo_both(c).wait_recv()
 
         def one(i, carry):
             u = 4 * c + i
@@ -386,7 +388,7 @@
 
     def send_copy(s, o):
         return remote(
-            sent_ref.at[s, o], all_ref.at[yz], send_sem.at[s, o], recv_sem.at[yz],
+            sent_ref.at[s, o], all_ref.at[yz], send_sem, recv_sem,
             (ty, tz + s // 2, lax.rem(s, 2), o),
         )
 
@@ -449,29 +451,31 @@
 
     lax.fori_loop(0, 8, pair, 0)
 
-    for s in range(4):
-        for o in range(4):
-
-            @pl.when(to_self(s, o))
-            def _():
-                own_copy(s, o).wait()
-
-            @pl.when(jnp.logical_not(to_self(s, o)))
-            def _():
-                send_copy(s, o).wait_send()
-
-    for c in range(PARTS):
-
-        def edges_left(c=c):
-            for side in range(2):
-                halo_copy(side, c).wait_send()
-
-        if c < 4:
-            edges_left()
-        else:
-            pl.when(odd)(edges_left)
-        if c >= 4:
-            each_line(c, lambda peer: line_copy(peer, c).wait_send())
+    def final(count):
+        both = all_ref.at[pl.ds(0, count)]
+        return remote(both, both, send_sem, recv_sem, at_line(lax.rem(me + 1, LINE)))
+
+    @pl.when(source == me)
+    def _():
+        own_copy(0, 0).wait()
+        final(PLANE - 1).wait_send()
+
+    @pl.when(source != me)
+    def _():
+        final(PLANE).wait_send()
+
+    for c in range(4):
+        halo_both(c).wait_send()
+    for c in (4, 5):
+
+        @pl.when(odd)
+        def _():
+            halo_both(c).wait_send()
+            line_all(c, 3).wait_send()
+
+        @pl.when(jnp.logical_not(odd))
+        def _():
+            line_all(c, 4).wait_send()
 
     @pl.when(odd)
     def _():
@@ -488,13 +492,13 @@
 
     each_piece(left)
 
-    for b in range(PLANE):
-
-        @pl.when(jnp.logical_not(jnp.logical_and(b == yz, source == me)))
-        def _():
-            remote(
-                sent_ref.at[0, 0], all_ref.at[b], send_sem.at[0, 0], recv_sem.at[b], (b // 4, b % 4, xlo, chan)
-            ).wait_recv()
+    @pl.when(source == me)
+    def _():
+        final(PLANE - 1).wait_recv()
+
+    @pl.when(source != me)
+    def _():
+        final(PLANE).wait_recv()
 
     result = lax.dot_general(
         all_ref[...].reshape(PLANE * 96, C),
@@ -507,7 +511,7 @@
 
     def out_copy(g):
         at = pl.ds(45 * g, 45)
-        return pltpu.make_async_copy(stage_ref.at[at], out_ref.at[at], out_sem.at[g])
+        return pltpu.make_async_copy(stage_ref.at[at], out_ref.at[at], out_sem)
 
     def store(g, carry):
         tiles = []
@@ -526,8 +530,7 @@
         return carry
 
     lax.fori_loop(0, OWN // 8, store, 0)
-    for g in range(OWN // 8):
-        out_copy(g).wait()
+    pltpu.make_async_copy(stage_ref, out_ref, out_sem).wait()
 
 
 def layer(src, reach, quads, fields, weight, basis, tables):
@@ -563,10 +566,10 @@
             pltpu.VMEM((PLANE, 96, C), bf16),
             pltpu.VMEM((PLANE * 96, 1536), bf16),
             pltpu.VMEM((12 * C, 128), jnp.float32),
-            dma((LINE, PARTS)), dma((LINE, PARTS)), dma((POLE,)), dma((POLE,)), dma((2, PARTS)), dma((2, PARTS)),
+            dma((PARTS,)), dma((PARTS,)), dma((POLE,)), dma((POLE,)), dma((PARTS,)), dma((PARTS,)),
             dma, dma, dma((3,)), dma((3,)), dma((4,)), dma((4,)), dma((3, 4)), dma((4, 3)), dma((3,)),
-            dma((4, 4)), dma((PLANE,)), pltpu.SemaphoreType.REGULAR,
-            pltpu.VMEM((OWN * MODES // 128, 8, 128), jnp.float32), dma((OWN // 8,)),
+            dma, dma, pltpu.SemaphoreType.REGULAR,
+            pltpu.VMEM((OWN * MODES // 128, 8, 128), jnp.float32), dma,
         ],
         compiler_params=pltpu.CompilerParams(
             collective_id=0, has_side_effects=True, vmem_limit_bytes=60 << 20

time: 72.3 us -> 71 us (0.982)
  Pallas kernels: 69.5 us -> 68.1 us
    pallas_call x1, Pallas kernels: 69.5 us -> 68.1 us  [layer(): pl.pallas_call(layer_kernel, out_shape=jax.ShapeDtypeStruct((OWN * MODES...]
where the time goes in v4:
time: 71 us; the launch traced here: 70.8 us
  Pallas kernels  68.1 us (96%)
  local copies, waits for them, and re-layouts  2.68 us (4%)
    pallas_call x1, Pallas kernels, layer(): pl.pallas_call(layer_kernel, out_shape=jax.ShapeDtypeStruct((OWN * MODES...  68.1 us
    unnamed x1, local copies, waits for them, and re-layouts  2.68 us

profile of v4, /device:TPU:103, one launch (start us, length us, event | category | flops | bytes accessed | tf_op | source)
XLA Modules:
  0.0 70.8 jit_solution(14302510209014390410)
XLA Ops:
  0.0 68.1 %shard_map.100 = f32[540,8,128]{2,1,0:T(8,128)} custom-call(s32[5,128]{1,0:T(8,128)} %bitcast.8, s32[5,128]{1,0:T(8,128)} %bitcast.9, f32[128]{0:T(128)} %quad_ref.1, bf16[45,12288]{1,0:T(8,128)(2,1)} %fields_ref.1, bf16[96,3456]{1,0:T(8,128)(2,1)} %weight_ref.1, f32[5,9,65,128]{3,2,1,0:T(8,128)} %basis_in.1, f32[96,1536]{1,0:T(8,128)} %constant.8.clone.p_in, ...), custom_call_target="tpu_custom_call" | custom-call | tf_op jit(solution)/shard_map/pallas_call | solution.py:542
  68.1 2.7 %copy.13 = f32[4,138240]{1,0:T(4,128)} copy(f32[4,138240]{1,0:T(4,128)} %bitcast.7) | data formatting | bytes 4423680
